TPU v7x, 256 devices: a whole 4x4x8 slice. The times are simulated.
256 devices in a mesh: fsdp: 32 (over z_hi, y, core), tp: 8 (over z_lo, x).
Axes of the slice: x: 4, y: 4, z: 8 (z_hi: 4, z_lo: 2; z = z_hi * 2 + z_lo), core: 2. Of those that a mesh axis runs over, the one named last changes fastest.
Arguments:
- normed: bfloat16 [32768, 8192], P('fsdp'), may hold values from -6 to 6
- kv_weight: bfloat16 [8192, 2048], P('fsdp', 'tp'), may hold values from -0.0625 to 0.0625
- kv_cotangent: bfloat16 [32768, 2048], P('fsdp', 'tp'), may hold values from -0.25 to 0.25
- first_moment: float32 [8192, 2048], P('fsdp', 'tp'), may hold values from -6 to 6
- second_moment: float32 [8192, 2048], P('fsdp', 'tp'), may hold values from 0.5 to 5
- cauchy_points: int32 [20], replicated, may hold values from 0 to 19, each once
Outputs:
- keys_values: bfloat16 [32768, 2048], P('fsdp', 'tp')
- new_first: float32 [8192, 2048], P('fsdp', 'tp')
- new_second: float32 [8192, 2048], P('fsdp', 'tp')
- parity: float32 [4, 2, 4096, 256], P(None, None, 'fsdp', 'tp')
Inputs may be any that keep to these rules, and one draw needn't show every extreme that they name: `cauchy_points`: each value once; the first 4 entries are the parity points, the other 16 the members' points in rank order.
All inputs are finite; a program needn't handle non-finite values.
Results may differ from a plain program's by a relative error of at most 0.001.
Values may be sent and summed in bfloat16 or wider, within the bound.
A program may use at most 192 MiB of HBM per device.

v0:
```python
import jax
import jax.numpy as jnp
from jax import lax
from jax.sharding import PartitionSpec as P

GROUP = 16
PARITY = 4


beta_first = 0.9
beta_second = 0.95


def from_partner(shard, axis, bit):
    return lax.ppermute(shard, axis, [(i, i ^ 1 << bit) for i in range(lax.axis_size(axis))])


def halve_rows(values, fsdp_index):
    half_rows = values.shape[2] // 2
    upper = fsdp_index // (1 << 0) % 2
    retained = lax.dynamic_slice_in_dim(values, upper * half_rows, half_rows, 2)
    outgoing = lax.dynamic_slice_in_dim(values, (1 - upper) * half_rows, half_rows, 2)
    values = retained + from_partner(outgoing, "fsdp", 0)
    return values


def local(normed, kv_weight, kv_cotangent, first_moment, second_moment, cauchy_points):
    contract = (((0,), (0,)), ((), ()))
    columns = normed
    projected = jnp.dot(
        columns,
        lax.all_gather(kv_weight, "fsdp", axis=0, tiled=True),
        preferred_element_type=jnp.float32,
    )
    keys_values = projected.astype(jnp.bfloat16)
    columns = normed
    gradient = lax.psum_scatter(
        lax.dot_general(columns, kv_cotangent, contract, preferred_element_type=jnp.float32),
        "fsdp",
        scatter_dimension=0,
        tiled=True,
    )
    new_first = beta_first * first_moment + (1.0 - beta_first) * gradient
    new_second = beta_second * second_moment + (1.0 - beta_second) * gradient * gradient
    points = cauchy_points.astype(jnp.float32)
    cauchy = 1.0 / (points[:PARITY, None] - points[None, PARITY:])
    tp_count = lax.axis_size("tp")
    group_rows = GROUP // tp_count
    fsdp_index = lax.axis_index("fsdp")
    payload = jnp.stack([new_first, new_second])
    member_rank = fsdp_index % group_rows * tp_count + lax.axis_index("tp")
    selector = (jnp.arange(GROUP, dtype=jnp.int32) == member_rank).astype(jnp.float32)
    column_weights = jnp.sum(cauchy * selector[None, :], axis=1)
    contribution = column_weights[:, None, None, None] * payload[None]
    summed = lax.psum_scatter(contribution, "tp", scatter_dimension=3, tiled=True)
    parity = halve_rows(summed, fsdp_index)
    return (keys_values, new_first, new_second, parity)


def solution(mesh):
    return jax.shard_map(
        local,
        mesh=mesh,
        in_specs=(
            P("fsdp", None),
            P("fsdp", "tp"),
            P("fsdp", "tp"),
            P("fsdp", "tp"),
            P("fsdp", "tp"),
            P(),
        ),
        out_specs=(P("fsdp", "tp"), P("fsdp", "tp"), P("fsdp", "tp"), P(None, None, "fsdp", "tp")),
        check_vma=False,
    )
```

profile of v0, /device:TPU:1, one launch (start us, length us, event | category | flops | bytes accessed | tf_op | source)
XLA Modules:
  0.0 275.5 jit_solution(3754259046699484786)
XLA Ops:
  7.2 0.0 copy-start
  7.2 0.0 reduce-scatter.3.cloned.1.call-start
  7.2 1.0 copy-done
  8.2 13.7 %fusion.1 = f32[8192,256]{1,0:T(8,128)} fusion(bf16[1024,8192]{1,0:T(8,128)(2,1)} %param.6, bf16[1024,256]{1,0:T(8,128)(2,1)S(1)} %copy-done), kind=kOutput, calls=%fused_computation.10 | convolution fusion | flops 4294967296 | bytes 25690112 | tf_op jit(solution)/shard_map/dot_general | solution.py:38
  22.0 0.0 copy-start.6
  22.0 0.0 copy-start.3
  22.0 0.0 copy-start.4
  22.0 0.0 reduce-scatter.3.cloned.1.call-update
  22.0 0.0 reduce-scatter.5.cloned.1.call-start
  22.0 0.6 copy-done.6
  22.6 0.1 slice.7
  22.7 0.2 multiply_reduce_fusion
  22.9 123.0 %reduce-scatter.3.cloned.1.call-done = f32[256,256]{1,0:T(8,128)} async-done(((f32[8192,256]{1,0:T(8,128)}), f32[256,256]{1,0:T(8,128)}) %reduce-scatter.3.cloned.1.call-update) | async-done | bytes 262160 | tf_op jit(solution)/shard_map/reduce_scatter | solution.py:37
  145.9 0.0 copy-done.3
  145.9 0.0 copy-done.4
  145.9 1.0 fusion
  146.9 0.0 copy-start.1
  146.9 0.0 copy-start.2
  147.0 0.2 copy.11
  147.2 1.6 broadcast_multiply_fusion
  148.8 0.0 reduce-scatter.5.cloned.1.call-update
  148.8 0.0 all-gather.2.cloned.1.call-start
  148.8 0.7 all-gather.2.cloned.1.call-update
  149.5 39.2 %reduce-scatter.5.cloned.1.call-done = f32[4,2,256,32]{2,3,1,0:T(8,128)} async-done(((f32[4,2,256,256]{2,3,1,0:T(8,128)}), f32[4,2,256,32]{2,3,1,0:T(8,128)}) %reduce-scatter.5.cloned.1.call-update) | async-done | bytes 262160 | tf_op jit(solution)/shard_map/reduce_scatter | solution.py:55
  188.7 0.9 constant_dynamic-slice_fusion
  189.6 0.0 copy-start.5
  189.7 5.9 %collective-permute-start = (f32[4,2,128,32]{2,3,1,0:T(8,128)S(1)}, f32[4,2,128,32]{2,3,1,0:T(8,128)S(1)}, u32[]{:S(2)}, u32[]{:S(2)}) collective-permute-start(f32[4,2,128,32]{2,3,1,0:T(8,128)S(1)} %constant_dynamic-slice_fusion), channel_id=1, source_target_pairs={{0,8},{8,0},{16,24},{24,16},{32,40},{40,32},{48,56},{56,48},{64,72... | collective-permute-start | bytes 393224 | tf_op jit(solution)/shard_map/ppermute | solution.py:15
  195.6 60.5 %all-gather.2.cloned.1.call-done = bf16[8192,256]{1,0:T(8,128)(2,1)} async-done(((bf16[256,256]{1,0:T(8,128)(2,1)}), bf16[8192,256]{1,0:T(8,128)(2,1)}) %all-gather.2.cloned.1.call-update) | async-done | bytes 4194320 | tf_op jit(solution)/shard_map/all_gather | solution.py:32
  256.0 12.2 %convolution_convert_fusion = bf16[1024,256]{1,0:T(8,128)(2,1)} fusion(bf16[1024,8192]{1,0:T(8,128)(2,1)} %param.6, bf16[8192,256]{1,0:T(8,128)(2,1)} %all-gather.2.cloned.1.call-done), kind=kOutput, calls=%fused_computation | convolution fusion | flops 4295229440 | bytes 21495808 | tf_op jit(solution)/shard_map/dot_general | solution.py:30
  268.2 0.0 copy-done.1
  268.3 0.0 copy-done.2
  268.3 0.0 collective-permute-done
  268.3 0.0 copy-done.5
  268.3 0.7 dynamic-slice_add_fusion
  (3 shorter events, 0.0 us)
Async XLA Ops:
  7.2 1.0 copy-start
  7.2 138.7 %reduce-scatter.3.cloned.1.call-start = ((), (), s32[]{:S(2)}) async-start(), calls=%async_computation.3 | async-start | bytes 8650752 | tf_op jit(solution)/shard_map/reduce_scatter | solution.py:37
  22.0 0.7 copy-start.6
  22.0 123.9 %copy-start.3 = (f32[256,256]{1,0:T(8,128)S(1)}, f32[256,256]{1,0:T(8,128)}, u32[]{:S(2)}) copy-start(f32[256,256]{1,0:T(8,128)} %param.10) | copy-start | bytes 786436
  22.0 123.9 %copy-start.4 = (f32[256,256]{1,0:T(8,128)S(1)}, f32[256,256]{1,0:T(8,128)}, u32[]{:S(2)}) copy-start(f32[256,256]{1,0:T(8,128)} %param.9) | copy-start | bytes 786436
  22.0 166.7 %reduce-scatter.5.cloned.1.call-start = ((), (), s32[]{:S(2)}) async-start(), calls=%async_computation.4 | async-start | bytes 2359296 | tf_op jit(solution)/shard_map/reduce_scatter | solution.py:55
  146.9 121.3 %copy-start.1 = (f32[256,256]{1,0:T(8,128)}, f32[256,256]{1,0:T(8,128)S(1)}, u32[]{:S(2)}) copy-start(f32[256,256]{1,0:T(8,128)S(1)} %get-tuple-element.4) | copy-start | bytes 786436
  146.9 121.3 %copy-start.2 = (f32[256,256]{1,0:T(8,128)}, f32[256,256]{1,0:T(8,128)S(1)}, u32[]{:S(2)}) copy-start(f32[256,256]{1,0:T(8,128)S(1)} %get-tuple-element.5) | copy-start | bytes 786436
  148.8 107.2 %all-gather.2.cloned.1.call-start = ((), (), s32[]{:S(2)}) async-start(), calls=%async_computation.2 | async-start | bytes 4325376 | tf_op jit(solution)/shard_map/all_gather | solution.py:32
  189.6 78.6 %copy-start.5 = (f32[4,2,256,32]{2,3,1,0:T(8,128)S(1)}, f32[4,2,256,32]{2,3,1,0:T(8,128)}, u32[]{:S(2)}) copy-start(f32[4,2,256,32]{2,3,1,0:T(8,128)} %reduce-scatter.5.cloned.1.call-done) | copy-start | bytes 786436
  189.7 78.6 %collective-permute-start = (f32[4,2,128,32]{2,3,1,0:T(8,128)S(1)}, f32[4,2,128,32]{2,3,1,0:T(8,128)S(1)}, u32[]{:S(2)}, u32[]{:S(2)}) collective-permute-start(f32[4,2,128,32]{2,3,1,0:T(8,128)S(1)} %constant_dynamic-slice_fusion), channel_id=1, source_target_pairs={{0,8},{8,0},{16,24},{24,16},{32,40},{40,32},{48,56},{56,48},{64,72... | collective-permute-start | bytes 393224 | tf_op jit(solution)/shard_map/ppermute | solution.py:15
Sparse Core Ops, SparseCore 0:
  22.1 123.7 reduce-scatter.2
  148.9 39.7 reduce-scatter.4
  191.3 64.6 all-gather.1
where the time goes:
time: 276 us; the launch traced here: 275 us
  waiting for transfers between devices  223 us (81%)
  matrix products  26 us (9%)
  between operations  13.8 us (5%)
  starting transfers between devices  6.01 us (2%)
  other arithmetic  3.5 us (1%)
  local copies, waits for them, and re-layouts  2.77 us (1%)
    reduce_scatter x1, waiting for transfers between devices, local(): lax.psum_scatter(lax.dot_general(columns, kv_cotangent, contract, preferr...  123 us
    all_gather x1, waiting for transfers between devices, local(): lax.all_gather(kv_weight, 'fsdp', axis=0, tiled=True)  60.5 us
    reduce_scatter x1, waiting for transfers between devices, local(): lax.psum_scatter(contribution, 'tp', scatter_dimension=3, tiled=True)  39.2 us
    dot_general x1, matrix products, local(): lax.dot_general(columns, kv_cotangent, contract, preferred_element_type=j...  13.7 us
    dot_general x1, matrix products, local(): jnp.dot(columns, lax.all_gather(kv_weight, 'fsdp', axis=0, tiled=True), p...  12.2 us
    ppermute x1, starting transfers between devices, from_partner(): lax.ppermute(shard, axis, [(i, i ^ 1 << bit) for i in range(lax.axis_size...  5.89 us
  transfers between devices with their start and end apart: 4, of which 3 were waited for; matrix products, arithmetic and copies ran while one was open for 5% of the time, Pallas kernels for 0%

commit v1 on v0

v1 whole, which is shorter than its diff:
```python
import functools

import jax
import jax.numpy as jnp
from jax import lax
from jax.experimental import pallas as pl
from jax.experimental.pallas import tpu as pltpu
from jax.sharding import PartitionSpec as P

MESH = pl.DeviceIdType.MESH
GROUP = 16
PARITY = 4
BETA_FIRST = 0.9
BETA_SECOND = 0.95
HOP = 3
FIRST = 3


def order(i):
    return i % 3 + 3 * ((3 - i) // 3)


def gray(i):
    return i + i // 2 - 2 * (i // 3)


def encode(x, out):
    n = x.shape[0]
    top = jnp.max(jnp.abs(x), axis=0, keepdims=True)
    power = jnp.ceil(jnp.log2(jnp.maximum(top, 1e-30)))
    scaled = jnp.round(x * jnp.exp2(15.0 - power))
    out[0:n, :] = jnp.clip(scaled, -32767.0, 32767.0).astype(jnp.int32).astype(jnp.int16)
    out[n : n + 16, :] = jnp.broadcast_to(power, (16, x.shape[1])).astype(jnp.int32).astype(jnp.int16)


def decode(ref):
    n = ref.shape[0] - 16
    power = ref[n : n + 16, :].astype(jnp.int32).astype(jnp.float32)[0:1, :]
    return ref[0:n, :].astype(jnp.int32).astype(jnp.float32) * jnp.exp2(power - 15.0)


def kernel(
    normed, w, cot, m1, m2, points,
    kv, nf, ns, par,
    nb, wb, cb, ct, mb, mt, sums, tmp, xs, xr, ys, yr, zs, zr, acc, ps, pr,
    n_sem, in_sem, w_sem, xs_sem, xr_sem, ys_sem, yr_sem, zs_sem, zr_sem,
    agr_sem, agy_sem, agz_sem, ags_sem, agp_sem, ps_sem, pr_sem,
):
    f, t = lax.axis_index("fsdp"), lax.axis_index("tp")
    core, chip = f % 2, f // 2
    y, z = chip % 4, chip // 4
    rank = core * 8 + t

    def at(dz, dy):
        return {"fsdp": (((z + dz) % 4) * 4 + (y + dy) % 4) * 2 + core}

    partner = {"fsdp": chip * 2 + 1 - core}
    y_to = (at(0, 1), at(0, 3))
    z_to = (at(1, 0), at(3, 0))

    def remote(src, dst, send, recv, device):
        return pltpu.make_async_remote_copy(
            src_ref=src, dst_ref=dst, send_sem=send, recv_sem=recv, device_id=device, device_id_type=MESH
        )

    def load_pair(j):
        oz, oy = order(j // 4), order(j % 4)
        column = pl.multiple_of((((z + oz) % 4) * 4 + (y + oy) % 4) * 512, 512)
        return pltpu.make_async_copy(normed.at[:, pl.ds(column, 512)], nb.at[oz * 4 + oy], n_sem.at[j])

    own_cot = pltpu.make_async_copy(cot, cb, in_sem.at[0])
    own_w = pltpu.make_async_copy(w, wb.at[0, core], in_sem.at[1])
    own_m1 = pltpu.make_async_copy(m1, mb.at[0], in_sem.at[2])
    own_m2 = pltpu.make_async_copy(m2, mb.at[1], in_sem.at[3])
    own_cot.start()
    own_w.start()
    for j in range(4):
        load_pair(j).start()
    own_m1.start()
    own_m2.start()

    barrier = pltpu.get_barrier_semaphore()
    for device in (*y_to, *z_to):
        pl.semaphore_signal(barrier, inc=1, device_id=device, device_id_type=MESH)
    for d in range(1, 16):
        peer = (rank + d) % 16
        pl.semaphore_signal(
            barrier, inc=1, device_id={"fsdp": chip * 2 + peer // 8, "tp": peer % 8}, device_id_type=MESH
        )
    own_cot.wait()
    ct[...] = cb[...].astype(jnp.float32).T.astype(jnp.bfloat16)
    acc[...] = jnp.zeros_like(acc)
    own_w.wait()
    pl.semaphore_wait(barrier, 19)

    def w_part(slot, part):
        return wb.at[slot, core] if part is None else wb.at[slot, core, pl.ds(part * 128, 128)]

    def y_copy(oz, oy, way, part):
        there = oz * 4 + (oy + (3 if way == 0 else 1)) % 4
        return remote(
            w_part(oz * 4 + oy, part),
            w_part(there, part),
            agy_sem.at[oz, way + (0 if part is None else 2)],
            agr_sem.at[there, part or 0],
            y_to[way],
        )

    def z_copy(oz, way, part):
        there = (oz + (3 if way == 0 else 1)) % 4 * 4
        return remote(
            w_part(oz * 4, part),
            w_part(there, part),
            agz_sem.at[way + (0 if part is None else 2)],
            agr_sem.at[there, part or 0],
            z_to[way],
        )

    def partner_copy(slot):
        return remote(wb.at[slot, core], wb.at[slot, core], ags_sem.at[slot], agp_sem.at[slot], partner)

    def partner_arrived(slot):
        block = wb.at[slot, 1 - core]
        remote(block, block, ags_sem.at[slot], agp_sem.at[slot], partner).wait_recv()

    def arrived(slot, part):
        block = w_part(slot, part)
        remote(block, block, agy_sem.at[0, 0], agr_sem.at[slot, part or 0], y_to[0]).wait_recv()

    def spread(oz):
        y_copy(oz, 0, 0, None).start()
        y_copy(oz, 0, 1, None).start()
        partner_copy(oz * 4).start()

    z_copy(0, 0, None).start()
    z_copy(0, 1, None).start()
    spread(0)

    def gather_z_near():
        arrived(12, None)
        z_copy(3, 0, 0).start()
        arrived(4, None)
        z_copy(1, 1, 1).start()
        spread(1)
        spread(3)

    def gather_z_far():
        arrived(8, 0)
        arrived(8, 1)
        spread(2)

    def gather_y(k):
        if k < 4:
            oz = gray(k)
            arrived(oz * 4 + 3, None)
            y_copy(oz, 3, 0, 0).start()
            arrived(oz * 4 + 1, None)
            y_copy(oz, 1, 1, 1).start()
            partner_copy(oz * 4 + 3).start()
            partner_copy(oz * 4 + 1).start()
        if k > 0:
            oz = gray(k - 1)
            arrived(oz * 4 + 2, 0)
            arrived(oz * 4 + 2, 1)
            partner_copy(oz * 4 + 2).start()

    def x_copy(slot):
        return remote(xs.at[slot], xr.at[slot], xs_sem.at[slot], xr_sem.at[slot], partner)

    def yh_copy(way, oz, s):
        return remote(
            ys.at[way, oz, s], yr.at[way, oz, s], ys_sem.at[way, oz, s], yr_sem.at[way, oz, s], y_to[way]
        )

    def zh_copy(way, s):
        return remote(zs.at[way, s], zr.at[way, s], zs_sem.at[way, s], zr_sem.at[way, s], z_to[way])

    def half(way):
        return slice(way * 128, way * 128 + 128)

    def gradient(j):
        slot = order(j // 4) * 4 + order(j % 4)

        @pl.when(j + 4 < 16)
        def _():
            load_pair(j + 4).start()

        load_pair(j).wait()
        pair = jnp.dot(ct[...], nb[slot], preferred_element_type=jnp.float32)
        tmp[0] = pair[:, 0:256]
        tmp[1] = pair[:, 256:512]
        encode(tmp[1 - core], xs.at[slot])
        x_copy(slot).start()
        sums[slot] = tmp[core]

    def add_partner(j):
        slot = order(j // 4) * 4 + order(j % 4)
        x_copy(slot).wait_recv()
        sums[slot] += decode(xr.at[slot])

    def y_hop(g, s):
        oz = order(g)
        for way in range(2):
            if s > 0:
                yh_copy(way, oz, s - 1).wait_recv()
            slot = oz * 4 + (3 - s if way == 0 else (s + 1) % 4)
            x = sums[slot, :, half(way)]
            if s > 0:
                x = x + decode(yr.at[way, oz, s - 1])
            if s < 3:
                encode(x, ys.at[way, oz, s])
                yh_copy(way, oz, s).start()
            else:
                sums[slot, :, half(way)] = x

    def z_hop(way, s):
        oz = 3 - s if way == 0 else s + 1
        x = sums[oz * 4, :, half(way)]
        if s > 0:
            zh_copy(way, s - 1).wait_recv()
            x = x + decode(zr.at[way, s - 1])
        encode(x, zs.at[way, s])
        zh_copy(way, s).start()

    def transpose_moments():
        own_m1.wait()
        own_m2.wait()
        mt[0] = mb[0].T
        mt[1] = mb[1].T

    def p_copy(d):
        peer = (rank + d) % 16
        return remote(
            ps.at[peer // 8, peer % 8],
            pr.at[rank],
            ps_sem.at[d],
            pr_sem.at[rank],
            {"fsdp": chip * 2 + peer // 8, "tp": peer % 8},
        )

    def update():
        for way in range(2):
            zh_copy(way, 2).wait_recv()
            g = sums[0, :, half(way)] + decode(zr.at[way, 2])
            first = BETA_FIRST * mt[0, :, half(way)] + (1.0 - BETA_FIRST) * g
            second = BETA_SECOND * mt[1, :, half(way)] + (1.0 - BETA_SECOND) * g * g
            mt[0, :, half(way)] = first
            mt[1, :, half(way)] = second
            ps[way, :, 0] = first.reshape(8, 32, 128)
            ps[way, :, 1] = second.reshape(8, 32, 128)
        lax.fori_loop(1, 16, lambda d, c: (p_copy(d).start(), c)[1], 0)
        pr[rank] = ps[core, t]
        nf[...] = mt[0].T
        ns[...] = mt[1].T

    def project(q):
        slot = gray(q // 4) * 4 + gray(q % 4)
        partner_arrived(slot)
        acc[...] += jnp.dot(nb[slot], wb[slot].reshape(512, 256), preferred_element_type=jnp.float32)

    def events(j, low, high):
        def when(step, what):
            if low <= step < high:

                @pl.when(j == step)
                def _():
                    what()

        for s in range(4):
            start = FIRST + HOP * s
            if start < high and start + 12 >= low:

                @pl.when((j >= start) & (j <= start + 12) & ((j + 16 - start) % 4 == 0))
                def _():
                    y_hop((j - start) // 4, s)

        done = FIRST + HOP * 3
        when(4, lambda: gather_y(0))
        when(6, gather_z_near)
        when(9, gather_z_far)
        when(10, lambda: gather_y(1))
        when(13, lambda: gather_y(2))
        when(16, lambda: gather_y(3))
        when(20, lambda: gather_y(4))
        when(8, transpose_moments)
        when(done, lambda: z_hop(0, 0))
        when(done + 4, lambda: z_hop(1, 0))
        when(done + 8, lambda: (z_hop(0, 1), z_hop(1, 1)))
        when(done + 12, lambda: (z_hop(0, 2), z_hop(1, 2)))
        when(done + 15, update)

    def first_loop(j, carry):
        gradient(j)

        @pl.when(j >= 2)
        def _():
            add_partner(j - 2)

        events(j, 0, 16)
        return carry

    lax.fori_loop(0, 16, first_loop, 0)
    add_partner(14)
    add_partner(15)

    def second_loop(j, carry):
        project(j - 16)
        events(j, 16, 32)
        return carry

    lax.fori_loop(16, 32, second_loop, 0)
    kv[...] = acc[...].astype(jnp.bfloat16)

    par[...] = jnp.zeros_like(par)

    def member(d, carry):
        r = (rank + 16 - d) % 16

        @pl.when(d > 0)
        def _():
            remote(ps.at[core, t], pr.at[r], ps_sem.at[d], pr_sem.at[r], partner).wait_recv()

        block = pr[r]
        for i in range(PARITY):
            gap = jnp.full((32, 128), points[i] - points[PARITY + r], jnp.int32).astype(jnp.float32)
            par[i] += (1.0 / gap) * block
        return carry

    lax.fori_loop(0, 16, member, 0)

    def sent_slot(slot, carry):
        x_copy(slot).wait_send()
        partner_copy(slot).wait_send()
        return carry

    lax.fori_loop(0, 16, sent_slot, 0)
    for way in range(2):
        for oz in range(4):
            y_copy(oz, 0, way, None).wait_send()
            y_copy(oz, 3 if way == 0 else 1, way, way).wait_send()
            for s in range(3):
                yh_copy(way, oz, s).wait_send()
        z_copy(0, way, None).wait_send()
        z_copy(3 if way == 0 else 1, way, way).wait_send()
        for s in range(3):
            zh_copy(way, s).wait_send()
    lax.fori_loop(1, 16, lambda d, c: (p_copy(d).wait_send(), c)[1], 0)


def local(normed, kv_weight, kv_cotangent, first_moment, second_moment, cauchy_points):
    anywhere = pl.BlockSpec(memory_space=pl.ANY)
    vmem = pl.BlockSpec(memory_space=pltpu.VMEM)
    dma = pltpu.SemaphoreType.DMA
    kv, nf, ns, par = pl.pallas_call(
        kernel,
        out_shape=(
            jax.ShapeDtypeStruct((1024, 256), jnp.bfloat16),
            jax.ShapeDtypeStruct((256, 256), jnp.float32),
            jax.ShapeDtypeStruct((256, 256), jnp.float32),
            jax.ShapeDtypeStruct((PARITY, 2, 32, 128), jnp.float32),
        ),
        in_specs=[anywhere] * 5 + [pl.BlockSpec(memory_space=pltpu.SMEM)],
        out_specs=(vmem,) * 4,
        scratch_shapes=[
            pltpu.VMEM((16, 1024, 512), jnp.bfloat16),
            pltpu.VMEM((16, 2, 256, 256), jnp.bfloat16),
            pltpu.VMEM((1024, 256), jnp.bfloat16),
            pltpu.VMEM((256, 1024), jnp.bfloat16),
            pltpu.VMEM((2, 256, 256), jnp.float32),
            pltpu.VMEM((2, 256, 256), jnp.float32),
            pltpu.VMEM((16, 256, 256), jnp.float32),
            pltpu.VMEM((2, 256, 256), jnp.float32),
            pltpu.VMEM((16, 272, 256), jnp.int16),
            pltpu.VMEM((16, 272, 256), jnp.int16),
            pltpu.VMEM((2, 4, 3, 272, 128), jnp.int16),
            pltpu.VMEM((2, 4, 3, 272, 128), jnp.int16),
            pltpu.VMEM((2, 3, 272, 128), jnp.int16),
            pltpu.VMEM((2, 3, 272, 128), jnp.int16),
            pltpu.VMEM((1024, 256), jnp.float32),
            pltpu.VMEM((2, 8, 2, 32, 128), jnp.float32),
            pltpu.VMEM((16, 2, 32, 128), jnp.float32),
            dma((16,)),
            dma((4,)),
            dma((1,)),
            dma((16,)),
            dma((16,)),
            dma((2, 4, 3)),
            dma((2, 4, 3)),
            dma((2, 3)),
            dma((2, 3)),
            dma((16, 2)),
            dma((4, 4)),
            dma((4,)),
            dma((16,)),
            dma((16,)),
            dma((16,)),
            dma((16,)),
        ],
        compiler_params=pltpu.CompilerParams(
            collective_id=0, has_side_effects=True, vmem_limit_bytes=60 * 1024 * 1024
        ),
    )(normed, kv_weight, kv_cotangent, first_moment, second_moment, cauchy_points)
    return kv, nf, ns, par.transpose(0, 1, 3, 2)


def solution(mesh):
    return jax.shard_map(
        local,
        mesh=mesh,
        in_specs=(
            P("fsdp", None),
            P("fsdp", "tp"),
            P("fsdp", "tp"),
            P("fsdp", "tp"),
            P("fsdp", "tp"),
            P(),
        ),
        out_specs=(P("fsdp", "tp"), P("fsdp", "tp"), P("fsdp", "tp"), P(None, None, "fsdp", "tp")),
        check_vma=False,
    )
```

time: 276 us -> 75.7 us (0.27)
  waiting for transfers between devices: 223 us -> 0 us
  Pallas kernels: 0 us -> 68 us
  matrix products: 26 us -> 0 us
  between operations: 13.8 us -> 0.64 us
  starting transfers between devices: 6.01 us -> 0 us
  local copies, waits for them, and re-layouts: 2.77 us -> 6.77 us
  other arithmetic: 3.5 us -> 0 us
    reduce_scatter x2 -> x0, waiting for transfers between devices: 162 us -> none  [the longest x1 123 us: local(): lax.psum_scatter(lax.dot_general(columns, kv_cotangent, contract, preferr...]
    pallas_call x0 -> x1, Pallas kernels: none -> 68 us  [local(): pl.pallas_call(kernel, out_shape=(jax.ShapeDtypeStruct((1024, 256), jnp.b...]
    all_gather x1 -> x0, waiting for transfers between devices: 60.5 us -> none  [local(): lax.all_gather(kv_weight, 'fsdp', axis=0, tiled=True)]
    dot_general x2 -> x0, matrix products: 26 us -> none  [the longest x1 13.7 us: local(): lax.dot_general(columns, kv_cotangent, contract, preferred_element_type=j...]
    ppermute x1 -> x0, starting transfers between devices: 5.89 us -> none  [from_partner(): lax.ppermute(shard, axis, [(i, i ^ 1 << bit) for i in range(lax.axis_size...]
    unnamed x14 -> x4, local copies, waits for them, and re-layouts: 1.59 us -> 6.77 us
  transfers between devices with their start and end apart: 4 -> 0, of which waited for: 3 -> 0; matrix products, arithmetic and copies ran while one was open for 5% -> 0% of each run, Pallas kernels for 0% -> 0%
where the time goes in v1:
time: 75.7 us; the launch traced here: 75.4 us
  Pallas kernels  68 us (90%)
  local copies, waits for them, and re-layouts  6.77 us (9%)
    pallas_call x1, Pallas kernels, local(): pl.pallas_call(kernel, out_shape=(jax.ShapeDtypeStruct((1024, 256), jnp.b...  68 us
    unnamed x4, local copies, waits for them, and re-layouts  6.77 us

profile of v1, /device:TPU:1, one launch (start us, length us, event | category | flops | bytes accessed | tf_op | source)
XLA Modules:
  0.0 75.4 jit_solution(17447376220214185069)
XLA Ops:
  0.6 68.0 %shard_map.93 = (bf16[1024,256]{1,0:T(8,128)(2,1)}, f32[256,256]{1,0:T(8,128)}, f32[256,256]{1,0:T(8,128)}, f32[4,2,32,128]{3,2,1,0:T(8,128)}) custom-call(bf16[1024,8192]{1,0:T(8,128)(2,1)} %normed.1, bf16[256,256]{1,0:T(8,128)(2,1)} %w.1, bf16[1024,256]{1,0:T(8,128)(2,1)} %cot.1, f32[256,256]{1,0:T(8,128)} %m1.1, f32[256,256]{1,0:T(8,128)} %m2.1, s32[20]{0:T(128)} %points.1), custom_call_target="tpu_custom_call" | custom-call | tf_op jit(solution)/shard_map/pallas_call | solution.py:354
  68.7 1.9 %copy.14 = bf16[1024,256]{1,0:T(8,128)(2,1)} copy(bf16[1024,256]{1,0:T(8,128)(2,1)} %get-tuple-element.16) | data formatting | bytes 1048576
  70.5 1.7 %copy.15 = f32[256,256]{1,0:T(8,128)} copy(f32[256,256]{1,0:T(8,128)} %get-tuple-element.17) | data formatting | bytes 524288
  72.2 1.7 %copy.16 = f32[256,256]{1,0:T(8,128)} copy(f32[256,256]{1,0:T(8,128)} %get-tuple-element.18) | data formatting | bytes 524288
  73.9 1.6 %copy.17 = f32[4,2,128,32]{2,3,1,0:T(8,128)} copy(f32[4,2,128,32]{2,3,1,0:T(8,128)} %bitcast.1) | data formatting | bytes 262144

commit v2 on v0

v2 whole, which is shorter than its diff:
```python
import jax
import jax.numpy as jnp
from jax import lax
from jax.experimental import pallas as pl
from jax.experimental.pallas import tpu as pltpu
from jax.sharding import PartitionSpec as P

MESH = pl.DeviceIdType.MESH
GROUP = 16
PARITY = 4
BETA_FIRST = 0.9
BETA_SECOND = 0.95
FULL = 32766.0 / 32768.0


ORDER = (2, 3, 1, 0)


def power_of(top):
    return jnp.ceil(jnp.log2(jnp.maximum(top, 1e-30)))


def to_code(x, power):
    return to_int16(jnp.round(x * (jnp.exp2(15.0 - power) * FULL)))


def step_of(power):
    return jnp.exp2(power - 15.0) * (1.0 / FULL)


def to_int16(x):
    return x.astype(jnp.int32).astype(jnp.int16)


def to_float(x):
    return x.astype(jnp.int32).astype(jnp.float32)


def encode(x, out):
    n = x.shape[0]
    power = power_of(jnp.max(jnp.abs(x), axis=0, keepdims=True))
    out[0:n, :] = to_code(x, power)
    out[n : n + 16, :] = to_int16(jnp.broadcast_to(power, (16, x.shape[1])))


def decode(ref):
    n = ref.shape[0] - 16
    power = to_float(ref[n : n + 16, :])[0:1, :]
    return to_float(ref[0:n, :]) * step_of(power)


def encode_blocks(x, kind, powers, out):
    blocks = x.reshape(8, 32, 128)
    power = power_of(jnp.max(jnp.abs(blocks), axis=1, keepdims=True))
    out[:, kind * 32 : kind * 32 + 32, :] = to_code(blocks, power)
    powers.append(power)


def encode_powers(powers, out):
    low = lax.broadcasted_iota(jnp.int32, (8, 16, 128), 1) < 8
    out[:, 64:80, :] = to_int16(jnp.where(low, powers[0], powers[1]))


def decode_block(ref):
    powers = to_float(ref[64:80, :])
    return [
        to_float(ref[kind * 32 : kind * 32 + 32, :]) * step_of(powers[kind * 8 : kind * 8 + 1, :])
        for kind in range(2)
    ]


def kernel(
    normed, w, cot, m1, m2, cauchy_points,
    kv, nf, ns, par,
    nb, wb, cb, ct, mb, mt, sums, tmp, xs, xr, ys, yr, zs, zr, acc, ps, pr, points,
    n_sem, in_sem, xs_sem, xr_sem, ys_sem, yr_sem, zs_sem, zr_sem,
    agr_sem, agy_sem, agz_sem, ags_sem, agp_sem, ps_sem, pr_sem,
):
    f, t = lax.axis_index("fsdp"), lax.axis_index("tp")
    core, chip = f & 1, f >> 1
    y, z = chip & 3, chip >> 2
    rank = core * 8 + t

    def at(dz, dy):
        return {"fsdp": ((((z + dz) & 3) << 2) + ((y + dy) & 3)) * 2 + core}

    def member_at(peer):
        return {"fsdp": chip * 2 + (peer >> 3), "tp": peer & 7}

    partner = {"fsdp": chip * 2 + 1 - core}
    y_to = (at(0, 1), at(0, 3))
    z_to = (at(1, 0), at(3, 0))

    def remote(src, dst, send, recv, device):
        return pltpu.make_async_remote_copy(
            src_ref=src, dst_ref=dst, send_sem=send, recv_sem=recv, device_id=device, device_id_type=MESH
        )

    def load_pair(slot, column):
        return pltpu.make_async_copy(normed.at[:, pl.ds(column, 512)], nb.at[slot], n_sem.at[slot])

    own_cot = pltpu.make_async_copy(cot, cb, in_sem.at[0])
    own_w = pltpu.make_async_copy(w, wb.at[15, core], in_sem.at[1])
    own_m1 = pltpu.make_async_copy(m1, mb.at[0], in_sem.at[2])
    own_m2 = pltpu.make_async_copy(m2, mb.at[1], in_sem.at[3])
    own_points = pltpu.make_async_copy(cauchy_points, points, in_sem.at[4])

    def w_part(slot, part):
        return wb.at[slot, core] if part is None else wb.at[slot, core, pl.ds(part * 128, 128)]

    def w_copy(slot, there, way, part, send, device):
        return remote(w_part(slot, part), w_part(there, part), send.at[slot, way], agr_sem.at[there, part or 0], device)

    def y_copy(base, place, way):
        to = {(3, 0): 1, (3, 1): 2, (1, 0): 0, (2, 1): 0}[place, way]
        return w_copy(base + place, base + to, way, None if place == 3 else way, agy_sem, y_to[way])

    def z_copy(slot, way):
        there = {(15, 0): 7, (15, 1): 11, (7, 0): 3, (11, 1): 3}[slot, way]
        return w_copy(slot, there, way, None if slot == 15 else way, agz_sem, z_to[way])

    def partner_copy(slot):
        return remote(wb.at[slot, core], wb.at[slot, core], ags_sem.at[slot], agp_sem.at[slot], partner)

    def partner_arrived(slot):
        block = wb.at[slot, 1 - core]
        remote(block, block, ags_sem.at[slot], agp_sem.at[slot], partner).wait_recv()

    def arrived(slot, part):
        block = w_part(slot, part)
        remote(block, block, agy_sem.at[0, 0], agr_sem.at[slot, part or 0], y_to[0]).wait_recv()

    def spread(base):
        y_copy(base, 3, 0).start()
        y_copy(base, 3, 1).start()

    def gather_start():
        own_w.wait()
        z_copy(15, 0).start()
        z_copy(15, 1).start()
        spread(12)
        partner_copy(15).start()

    def gather_z_near():
        arrived(7, None)
        z_copy(7, 0).start()
        arrived(11, None)
        z_copy(11, 1).start()
        partner_copy(7).start()
        partner_copy(11).start()

    def gather_z_far():
        arrived(3, 0)
        arrived(3, 1)
        partner_copy(3).start()

    def gather_y_near(base):
        arrived(base + 1, None)
        y_copy(base, 1, 0).start()
        arrived(base + 2, None)
        y_copy(base, 2, 1).start()
        partner_copy(base + 1).start()
        partner_copy(base + 2).start()

    def gather_y_far(base):
        arrived(base, 0)
        arrived(base, 1)
        partner_copy(base).start()

    def x_copy(slot):
        return remote(xs.at[slot], xr.at[slot], xs_sem.at[slot], xr_sem.at[slot], partner)

    def ysum_copy(way, g, s):
        return remote(ys.at[way, g, s], yr.at[way, g, s], ys_sem.at[way, g, s], yr_sem.at[way, g, s], y_to[way])

    def zsum_copy(way, s):
        return remote(zs.at[way, s], zr.at[way, s], zs_sem.at[way, s], zr_sem.at[way, s], z_to[way])

    def half(way):
        return slice(way * 128, way * 128 + 128)

    def gradient(j):
        load_pair(j, 0).wait()
        pair = jnp.dot(ct[...], nb[j], preferred_element_type=jnp.float32)
        tmp[0] = pair[:, 0:256]
        tmp[1] = pair[:, 256:512]
        encode(tmp[1 - core], xs.at[j])

        @pl.when(j == 0)
        def _():
            pl.semaphore_wait(barrier, 19)
            gather_start()

        x_copy(j).start()
        sums[j] = tmp[core]

    def add_partner(j):
        x_copy(j).wait_recv()
        sums[j] += decode(xr.at[j])

    def y_sum(g, s):
        base = g * 4
        for way in range(2):
            near = base + 2 - way
            if s == 0:
                encode(sums[base, :, half(way)], ys.at[way, g, 0])
            elif s == 1:
                encode(sums[near, :, half(1 - way)], ys.at[way, g, 1])
            elif s == 2:
                ysum_copy(way, g, 0).wait_recv()
                encode(sums[near, :, half(way)] + decode(yr.at[way, g, 0]), ys.at[way, g, 2])
            else:
                ysum_copy(1 - way, g, 1).wait_recv()
                ysum_copy(way, g, 2).wait_recv()
                sums[base + 3, :, half(way)] += decode(yr.at[1 - way, g, 1]) + decode(yr.at[way, g, 2])
            if s < 3:
                ysum_copy(way, g, s).start()

    def z_antipode():
        for way in range(2):
            encode(sums[3, :, half(way)], zs.at[way, 0])
            zsum_copy(way, 0).start()

    def z_free(way):
        encode(sums[11 if way == 0 else 7, :, half(1 - way)], zs.at[way, 1])
        zsum_copy(way, 1).start()

    def z_joined(way):
        zsum_copy(way, 0).wait_recv()
        encode(sums[11 if way == 0 else 7, :, half(way)] + decode(zr.at[way, 0]), zs.at[way, 2])
        zsum_copy(way, 2).start()

    def transpose_moments():
        own_m1.wait()
        own_m2.wait()
        own_points.wait()
        mt[0] = mb[0].T
        mt[1] = mb[1].T

    def p_copy(d):
        peer = (rank + d) & 15
        return remote(ps.at[peer >> 3, peer & 7], pr.at[rank], ps_sem.at[d], pr_sem.at[rank], member_at(peer))

    def update():
        for way in range(2):
            zsum_copy(1 - way, 1).wait_recv()
            zsum_copy(way, 2).wait_recv()
            g = sums[15, :, half(way)] + (decode(zr.at[1 - way, 1]) + decode(zr.at[way, 2]))
            first = BETA_FIRST * mt[0, :, half(way)] + (1.0 - BETA_FIRST) * g
            second = BETA_SECOND * mt[1, :, half(way)] + (1.0 - BETA_SECOND) * g * g
            mt[0, :, half(way)] = first
            mt[1, :, half(way)] = second
            powers = []
            encode_blocks(first, 0, powers, ps.at[way])
            encode_blocks(second, 1, powers, ps.at[way])
            encode_powers(powers, ps.at[way])
        lax.fori_loop(1, 16, lambda d, c: (p_copy(d).start(), c)[1], 0)
        pr[rank] = ps[core, t]
        nf[...] = mt[0].T
        ns[...] = mt[1].T

    def project(slot):
        partner_arrived(slot)
        acc[...] += jnp.dot(nb[slot], wb[slot].reshape(512, 256), preferred_element_type=jnp.float32)

    actions = {
        "near_0": lambda: gather_y_near(12),
        "far_0": lambda: gather_y_far(12),
        "z_near": gather_z_near,
        "z_far": gather_z_far,
        "moments": transpose_moments,
        "z_antipode": z_antipode,
        "z_free_1": lambda: z_free(1),
        "z_joined_1": lambda: z_joined(1),
        "z_free_0": lambda: z_free(0),
        "z_joined_0": lambda: z_joined(0),
        "spread_1": lambda: spread(8),
        "spread_2": lambda: spread(4),
        "spread_3": lambda: spread(0),
    }

    def events(j, low, high):
        for s in range(4):
            start = Y_STEPS[s]
            if start < high and start + 12 >= low:

                @pl.when((j >= start) & (j <= start + 12) & (((j - start) & 3) == 0))
                def _():
                    y_sum((j - start) >> 2, s)

        for step, names in STEPS.items():
            if low <= step < high:

                @pl.when(j == step)
                def _():
                    for name in names:
                        actions[name]()

    own_cot.start()
    rows = [((z + oz) & 3) << 11 for oz in ORDER]
    places = [((y + oy) & 3) << 9 for oy in ORDER]
    loads = [load_pair(4 * g + i, pl.multiple_of(rows[g] + places[i], 512)) for g in range(4) for i in range(4)]
    loads[0].start()
    own_w.start()
    for load in loads[1:]:
        load.start()
    own_m1.start()
    own_m2.start()
    own_points.start()

    barrier = pltpu.get_barrier_semaphore()
    for device in (*y_to, *z_to):
        pl.semaphore_signal(barrier, inc=1, device_id=device, device_id_type=MESH)
    for d in range(1, 16):
        pl.semaphore_signal(barrier, inc=1, device_id=member_at((rank + d) & 15), device_id_type=MESH)
    own_cot.wait()
    ct[...] = cb[...].astype(jnp.float32).T.astype(jnp.bfloat16)

    def first_loop(j, carry):
        gradient(j)

        @pl.when(j >= 2)
        def _():
            add_partner(j - 2)

        events(j, 0, 16)
        return carry

    lax.fori_loop(0, 16, first_loop, 0)
    acc[...] = jnp.zeros_like(acc)
    par[...] = jnp.zeros_like(par)

    def second_loop(j, carry):
        @pl.when(j < 18)
        def _():
            add_partner(j - 2)

        events(j, 16, LAST)

        @pl.when((j >= PROJECT) & (j < PROJECT + 4))
        def _():
            project(15 + PROJECT - j)

        return carry

    lax.fori_loop(16, LAST, second_loop, 0)
    update()

    def near_loop(k, carry):
        base = 12 - 4 * k
        gather_y_near(base)

        def three(i, inner):
            project(base + 3 - i)
            return inner

        return lax.fori_loop(0, 3, three, carry)

    def far_loop(k, carry):
        gather_y_far(12 - 4 * k)
        project(12 - 4 * k)
        return carry

    lax.fori_loop(1, 4, near_loop, 0)
    lax.fori_loop(1, 4, far_loop, 0)
    kv[...] = acc[...].astype(jnp.bfloat16)

    def member(d, carry):
        r = (rank + 16 - d) & 15

        @pl.when(d > 0)
        def _():
            remote(ps.at[core, t], pr.at[r], ps_sem.at[d], pr_sem.at[r], partner).wait_recv()

        blocks = decode_block(pr.at[r])
        for i in range(PARITY):
            gap = jnp.full((32, 128), points[i] - points[PARITY + r], jnp.int32).astype(jnp.float32)
            weight = 1.0 / gap
            for kind in range(2):
                par[i, kind] += weight * blocks[kind]
        return carry

    lax.fori_loop(0, 16, member, 0)

    def sent_slot(slot, carry):
        x_copy(slot).wait_send()
        partner_copy(slot).wait_send()
        return carry

    def sent_group(g, carry):
        for way in range(2):
            y_copy(4 * g, 3, way).wait_send()
            y_copy(4 * g, 1 + way, way).wait_send()
            for s in range(3):
                ysum_copy(way, g, s).wait_send()
        return carry

    lax.fori_loop(0, 16, sent_slot, 0)
    lax.fori_loop(0, 4, sent_group, 0)
    for way in range(2):
        z_copy(15, way).wait_send()
        z_copy(7 if way == 0 else 11, way).wait_send()
        for s in range(3):
            zsum_copy(way, s).wait_send()
    lax.fori_loop(1, 16, lambda d, c: (p_copy(d).wait_send(), c)[1], 0)


Y_STEPS = (2, 4, 6, 10)
STEPS = {
    5: ("near_0",),
    8: ("z_near", "moments"),
    9: ("far_0",),
    10: ("z_antipode",),
    13: ("z_far",),
    14: ("z_free_1",),
    16: ("z_joined_1",),
    18: ("z_free_0", "z_joined_0", "spread_1", "spread_2", "spread_3"),
}
PROJECT = 17
LAST = 23


def hand_out(*refs):
    half = len(refs) // 2
    for source, target in zip(refs[:half], refs[half:]):
        target[...] = source[...]


def local(normed, kv_weight, kv_cotangent, first_moment, second_moment, cauchy_points):
    hbm = pl.BlockSpec(memory_space=pltpu.HBM)
    vmem = pl.BlockSpec(memory_space=pltpu.VMEM)
    dma = pltpu.SemaphoreType.DMA
    shapes = (
        jax.ShapeDtypeStruct((1024, 256), jnp.bfloat16),
        jax.ShapeDtypeStruct((256, 256), jnp.float32),
        jax.ShapeDtypeStruct((256, 256), jnp.float32),
        jax.ShapeDtypeStruct((PARITY, 2, 32, 128), jnp.float32),
    )
    results = pl.pallas_call(
        kernel,
        out_shape=shapes,
        in_specs=[hbm] * 6,
        out_specs=(vmem,) * 4,
        scratch_shapes=[
            pltpu.VMEM((16, 1024, 512), jnp.bfloat16),
            pltpu.VMEM((16, 2, 256, 256), jnp.bfloat16),
            pltpu.VMEM((1024, 256), jnp.bfloat16),
            pltpu.VMEM((256, 1024), jnp.bfloat16),
            pltpu.VMEM((2, 256, 256), jnp.float32),
            pltpu.VMEM((2, 256, 256), jnp.float32),
            pltpu.VMEM((16, 256, 256), jnp.float32),
            pltpu.VMEM((2, 256, 256), jnp.float32),
            pltpu.VMEM((16, 272, 256), jnp.int16),
            pltpu.VMEM((16, 272, 256), jnp.int16),
            pltpu.VMEM((2, 4, 3, 272, 128), jnp.int16),
            pltpu.VMEM((2, 4, 3, 272, 128), jnp.int16),
            pltpu.VMEM((2, 3, 272, 128), jnp.int16),
            pltpu.VMEM((2, 3, 272, 128), jnp.int16),
            pltpu.VMEM((1024, 256), jnp.float32),
            pltpu.VMEM((2, 8, 80, 128), jnp.int16),
            pltpu.VMEM((16, 80, 128), jnp.int16),
            pltpu.SMEM((20,), jnp.int32),
            dma((16,)),
            dma((5,)),
            dma((16,)),
            dma((16,)),
            dma((2, 4, 3)),
            dma((2, 4, 3)),
            dma((2, 3)),
            dma((2, 3)),
            dma((16, 2)),
            dma((16, 2)),
            dma((16, 2)),
            dma((16,)),
            dma((16,)),
            dma((16,)),
            dma((16,)),
        ],
        compiler_params=pltpu.CompilerParams(
            collective_id=0, has_side_effects=True, vmem_limit_bytes=46 * 1024 * 1024
        ),
    )(*[pltpu.with_memory_space_constraint(v, pltpu.HBM) for v in (normed, kv_weight, kv_cotangent, first_moment, second_moment, cauchy_points)])
    kv, nf, ns, par = pl.pallas_call(
        hand_out,
        out_shape=shapes,
        in_specs=[vmem] * 4,
        out_specs=(vmem,) * 4,
        compiler_params=pltpu.CompilerParams(vmem_limit_bytes=8 * 1024 * 1024),
    )(*results)
    return kv, nf, ns, par.transpose(0, 1, 3, 2)


def solution(mesh):
    return jax.shard_map(
        local,
        mesh=mesh,
        in_specs=(
            P("fsdp", None),
            P("fsdp", "tp"),
            P("fsdp", "tp"),
            P("fsdp", "tp"),
            P("fsdp", "tp"),
            P(),
        ),
        out_specs=(P("fsdp", "tp"), P("fsdp", "tp"), P("fsdp", "tp"), P(None, None, "fsdp", "tp")),
        check_vma=False,
    )
```

time: 276 us -> 58.2 us (0.21)
  waiting for transfers between devices: 223 us -> 0 us
  Pallas kernels: 0 us -> 57.5 us
  matrix products: 26 us -> 0 us
  between operations: 13.8 us -> 0.64 us
  starting transfers between devices: 6.01 us -> 0 us
  other arithmetic: 3.5 us -> 0 us
  local copies, waits for them, and re-layouts: 2.77 us -> 0 us
    reduce_scatter x2 -> x0, waiting for transfers between devices: 162 us -> none  [the longest x1 123 us: local(): lax.psum_scatter(lax.dot_general(columns, kv_cotangent, contract, preferr...]
    all_gather x1 -> x0, waiting for transfers between devices: 60.5 us -> none  [local(): lax.all_gather(kv_weight, 'fsdp', axis=0, tiled=True)]
    pallas_call x0 -> x2, Pallas kernels: none -> 57.5 us  [the longest x1 56.4 us: local(): pl.pallas_call(kernel, out_shape=shapes, in_specs=[hbm] * 6, out_specs=(v...]
    dot_general x2 -> x0, matrix products: 26 us -> none  [the longest x1 13.7 us: local(): lax.dot_general(columns, kv_cotangent, contract, preferred_element_type=j...]
    ppermute x1 -> x0, starting transfers between devices: 5.89 us -> none  [from_partner(): lax.ppermute(shard, axis, [(i, i ^ 1 << bit) for i in range(lax.axis_size...]
  transfers between devices with their start and end apart: 4 -> 0, of which waited for: 3 -> 0; matrix products, arithmetic and copies ran while one was open for 5% -> 0% of each run, Pallas kernels for 0% -> 0%
where the time goes in v2:
time: 58.2 us
  Pallas kernels  57.5 us (99%)
  between operations  0.64 us (1%)
    pallas_call x1, Pallas kernels, local(): pl.pallas_call(kernel, out_shape=shapes, in_specs=[hbm] * 6, out_specs=(v...  56.4 us

profile of v2, /device:TPU:1, one launch (start us, length us, event | category | flops | bytes accessed | tf_op | source)
XLA Modules:
  0.0 58.2 jit_solution(10760064798105521045)
XLA Ops:
  0.6 56.4 %shard_map.93 = (bf16[1024,256]{1,0:T(8,128)(2,1)S(1)}, f32[256,256]{1,0:T(8,128)S(1)}, f32[256,256]{1,0:T(8,128)S(1)}, f32[4,2,32,128]{3,2,1,0:T(8,128)S(1)}) custom-call(bf16[1024,8192]{1,0:T(8,128)(2,1)} %normed.1, bf16[256,256]{1,0:T(8,128)(2,1)} %w.1, bf16[1024,256]{1,0:T(8,128)(2,1)} %cot.1, f32[256,256]{1,0:T(8,128)} %m1.1, f32[256,256]{1,0:T(8,128)} %m2.1, ...), custom_call_target="tpu_custom_call" | custom-call | tf_op jit(solution)/shard_map/pallas_call | solution.py:439
  57.1 1.1 %shard_map.94 = (bf16[1024,256]{1,0:T(8,128)(2,1)}, f32[256,256]{1,0:T(8,128)}, f32[256,256]{1,0:T(8,128)}, f32[4,2,32,128]{3,2,1,0:T(8,128)}) custom-call(bf16[1024,256]{1,0:T(8,128)(2,1)S(1)} %get-tuple-element.12.refs_0_, f32[256,256]{1,0:T(8,128)S(1)} %get-tuple-element.13.refs_1_, f32[256,256]{1,0:T(8,128)S(1)} %get-tuple-element.14.refs_2_, ...), custom_call_target="tpu_custom_call" | custom-call | tf_op jit(solution)/shard_map/pallas_call | solution.py:483

commit v3 on v2

--- a/solution.py
+++ b/solution.py
@@ -13,7 +13,13 @@
 FULL = 32766.0 / 32768.0
 
 
-ORDER = (2, 3, 1, 0)
+SEQUENCE = (
+    *((2, 2), (2, 3), (2, 1), (2, 0)),
+    *((1, 2), (3, 2), (1, 3), (3, 3), (1, 1), (3, 1), (1, 0), (3, 0)),
+    *((0, 2), (0, 3), (0, 1), (0, 0)),
+)
+SLOT = {chip: slot for slot, chip in enumerate(SEQUENCE)}
+HALVES = ((2, 2), (1, 3), (3, 1), (0, 0))
 
 
 def power_of(top):
@@ -72,7 +78,7 @@
 def kernel(
     normed, w, cot, m1, m2, cauchy_points,
     kv, nf, ns, par,
-    nb, wb, cb, ct, mb, mt, sums, tmp, xs, xr, ys, yr, zs, zr, acc, ps, pr, points,
+    nb, wb, cb, ct, mb, mt, sums, xs, xr, ys, yr, zs, zr, acc, ps, pr, points,
     n_sem, in_sem, xs_sem, xr_sem, ys_sem, yr_sem, zs_sem, zr_sem,
     agr_sem, agy_sem, agz_sem, ags_sem, agp_sem, ps_sem, pr_sem,
 ):
@@ -100,7 +106,7 @@
         return pltpu.make_async_copy(normed.at[:, pl.ds(column, 512)], nb.at[slot], n_sem.at[slot])
 
     own_cot = pltpu.make_async_copy(cot, cb, in_sem.at[0])
-    own_w = pltpu.make_async_copy(w, wb.at[15, core], in_sem.at[1])
+    own_w = pltpu.make_async_copy(w, wb.at[SLOT[0, 0], core], in_sem.at[1])
     own_m1 = pltpu.make_async_copy(m1, mb.at[0], in_sem.at[2])
     own_m2 = pltpu.make_async_copy(m2, mb.at[1], in_sem.at[3])
     own_points = pltpu.make_async_copy(cauchy_points, points, in_sem.at[4])
@@ -111,13 +117,15 @@
     def w_copy(slot, there, way, part, send, device):
         return remote(w_part(slot, part), w_part(there, part), send.at[slot, way], agr_sem.at[there, part or 0], device)
 
-    def y_copy(base, place, way):
-        to = {(3, 0): 1, (3, 1): 2, (1, 0): 0, (2, 1): 0}[place, way]
-        return w_copy(base + place, base + to, way, None if place == 3 else way, agy_sem, y_to[way])
-
-    def z_copy(slot, way):
-        there = {(15, 0): 7, (15, 1): 11, (7, 0): 3, (11, 1): 3}[slot, way]
-        return w_copy(slot, there, way, None if slot == 15 else way, agz_sem, z_to[way])
+    onward = {(0, 0): 3, (0, 1): 1, (3, 0): 2, (1, 1): 2}
+
+    def y_copy(oz, oy, way):
+        there = SLOT[oz, onward[oy, way]]
+        return w_copy(SLOT[oz, oy], there, way, way if oy else None, agy_sem, y_to[way])
+
+    def z_copy(oz, way):
+        there = SLOT[onward[oz, way], 0]
+        return w_copy(SLOT[oz, 0], there, way, way if oz else None, agz_sem, z_to[way])
 
     def partner_copy(slot):
         return remote(wb.at[slot, core], wb.at[slot, core], ags_sem.at[slot], agp_sem.at[slot], partner)
@@ -130,42 +138,42 @@
         block = w_part(slot, part)
         remote(block, block, agy_sem.at[0, 0], agr_sem.at[slot, part or 0], y_to[0]).wait_recv()
 
-    def spread(base):
-        y_copy(base, 3, 0).start()
-        y_copy(base, 3, 1).start()
+    def spread(oz):
+        y_copy(oz, 0, 0).start()
+        y_copy(oz, 0, 1).start()
 
     def gather_start():
         own_w.wait()
-        z_copy(15, 0).start()
-        z_copy(15, 1).start()
-        spread(12)
-        partner_copy(15).start()
-
-    def gather_z_near():
-        arrived(7, None)
-        z_copy(7, 0).start()
-        arrived(11, None)
-        z_copy(11, 1).start()
-        partner_copy(7).start()
-        partner_copy(11).start()
-
-    def gather_z_far():
-        arrived(3, 0)
-        arrived(3, 1)
-        partner_copy(3).start()
-
-    def gather_y_near(base):
-        arrived(base + 1, None)
-        y_copy(base, 1, 0).start()
-        arrived(base + 2, None)
-        y_copy(base, 2, 1).start()
-        partner_copy(base + 1).start()
-        partner_copy(base + 2).start()
-
-    def gather_y_far(base):
-        arrived(base, 0)
-        arrived(base, 1)
-        partner_copy(base).start()
+        z_copy(0, 0).start()
+        z_copy(0, 1).start()
+        spread(0)
+        partner_copy(SLOT[0, 0]).start()
+
+    def z_near():
+        arrived(SLOT[3, 0], None)
+        z_copy(3, 0).start()
+        arrived(SLOT[1, 0], None)
+        z_copy(1, 1).start()
+        partner_copy(SLOT[3, 0]).start()
+        partner_copy(SLOT[1, 0]).start()
+
+    def z_far():
+        arrived(SLOT[2, 0], 0)
+        arrived(SLOT[2, 0], 1)
+        partner_copy(SLOT[2, 0]).start()
+
+    def y_near(oz):
+        arrived(SLOT[oz, 3], None)
+        y_copy(oz, 3, 0).start()
+        arrived(SLOT[oz, 1], None)
+        y_copy(oz, 1, 1).start()
+        partner_copy(SLOT[oz, 3]).start()
+        partner_copy(SLOT[oz, 1]).start()
+
+    def y_far(oz):
+        arrived(SLOT[oz, 2], 0)
+        arrived(SLOT[oz, 2], 1)
+        partner_copy(SLOT[oz, 2]).start()
 
     def x_copy(slot):
         return remote(xs.at[slot], xr.at[slot], xs_sem.at[slot], xr_sem.at[slot], partner)
@@ -182,9 +190,9 @@
     def gradient(j):
         load_pair(j, 0).wait()
         pair = jnp.dot(ct[...], nb[j], preferred_element_type=jnp.float32)
-        tmp[0] = pair[:, 0:256]
-        tmp[1] = pair[:, 256:512]
-        encode(tmp[1 - core], xs.at[j])
+        sums[j, 0] = pair[:, 0:256]
+        sums[j, 1] = pair[:, 256:512]
+        encode(sums[j, 1 - core], xs.at[j])
 
         @pl.when(j == 0)
         def _():
@@ -192,43 +200,38 @@
             gather_start()
 
         x_copy(j).start()
-        sums[j] = tmp[core]
 
     def add_partner(j):
         x_copy(j).wait_recv()
-        sums[j] += decode(xr.at[j])
+        sums[j, core] += decode(xr.at[j])
 
     def y_sum(g, s):
-        base = g * 4
         for way in range(2):
-            near = base + 2 - way
-            if s == 0:
-                encode(sums[base, :, half(way)], ys.at[way, g, 0])
-            elif s == 1:
-                encode(sums[near, :, half(1 - way)], ys.at[way, g, 1])
-            elif s == 2:
+            part = 1 - way if s == 1 else way
+            oy = (2, 1 if way == 0 else 3, 1 if way == 0 else 3, 0)[s]
+            slot = SLOT[HALVES[g][part], oy]
+            x = sums[slot, core, :, half(part)]
+            if s == 2:
                 ysum_copy(way, g, 0).wait_recv()
-                encode(sums[near, :, half(way)] + decode(yr.at[way, g, 0]), ys.at[way, g, 2])
-            else:
+                x = x + decode(yr.at[way, g, 0])
+            if s == 3:
                 ysum_copy(1 - way, g, 1).wait_recv()
                 ysum_copy(way, g, 2).wait_recv()
-                sums[base + 3, :, half(way)] += decode(yr.at[1 - way, g, 1]) + decode(yr.at[way, g, 2])
-            if s < 3:
+                sums[slot, core, :, half(part)] = x + (decode(yr.at[1 - way, g, 1]) + decode(yr.at[way, g, 2]))
+            else:
+                encode(x, ys.at[way, g, s])
                 ysum_copy(way, g, s).start()
 
-    def z_antipode():
+    def z_sum(s):
         for way in range(2):
-            encode(sums[3, :, half(way)], zs.at[way, 0])
-            zsum_copy(way, 0).start()
-
-    def z_free(way):
-        encode(sums[11 if way == 0 else 7, :, half(1 - way)], zs.at[way, 1])
-        zsum_copy(way, 1).start()
-
-    def z_joined(way):
-        zsum_copy(way, 0).wait_recv()
-        encode(sums[11 if way == 0 else 7, :, half(way)] + decode(zr.at[way, 0]), zs.at[way, 2])
-        zsum_copy(way, 2).start()
+            part = 1 - way if s == 1 else way
+            oz = 2 if s == 0 else 1 if way == 0 else 3
+            x = sums[SLOT[oz, 0], core, :, half(part)]
+            if s == 2:
+                zsum_copy(way, 0).wait_recv()
+                x = x + decode(zr.at[way, 0])
+            encode(x, zs.at[way, s])
+            zsum_copy(way, s).start()
 
     def transpose_moments():
         own_m1.wait()
@@ -245,7 +248,7 @@
         for way in range(2):
             zsum_copy(1 - way, 1).wait_recv()
             zsum_copy(way, 2).wait_recv()
-            g = sums[15, :, half(way)] + (decode(zr.at[1 - way, 1]) + decode(zr.at[way, 2]))
+            g = sums[SLOT[0, 0], core, :, half(way)] + (decode(zr.at[1 - way, 1]) + decode(zr.at[way, 2]))
             first = BETA_FIRST * mt[0, :, half(way)] + (1.0 - BETA_FIRST) * g
             second = BETA_SECOND * mt[1, :, half(way)] + (1.0 - BETA_SECOND) * g * g
             mt[0, :, half(way)] = first
@@ -263,43 +266,28 @@
         partner_arrived(slot)
         acc[...] += jnp.dot(nb[slot], wb[slot].reshape(512, 256), preferred_element_type=jnp.float32)
 
-    actions = {
-        "near_0": lambda: gather_y_near(12),
-        "far_0": lambda: gather_y_far(12),
-        "z_near": gather_z_near,
-        "z_far": gather_z_far,
-        "moments": transpose_moments,
-        "z_antipode": z_antipode,
-        "z_free_1": lambda: z_free(1),
-        "z_joined_1": lambda: z_joined(1),
-        "z_free_0": lambda: z_free(0),
-        "z_joined_0": lambda: z_joined(0),
-        "spread_1": lambda: spread(8),
-        "spread_2": lambda: spread(4),
-        "spread_3": lambda: spread(0),
-    }
+    actions = {"z_near": z_near, "z_far": z_far, "moments": transpose_moments, "update": update}
+    for k in range(4):
+        actions[f"spread_{k}"] = lambda k=k: spread(k)
+        actions[f"near_{k}"] = lambda k=k: y_near(k)
+        actions[f"far_{k}"] = lambda k=k: y_far(k)
+        actions[f"z_{k}"] = lambda k=k: z_sum(k)
+        for s in range(4):
+            actions[f"y_{k}_{s}"] = lambda k=k, s=s: y_sum(k, s)
 
     def events(j, low, high):
-        for s in range(4):
-            start = Y_STEPS[s]
-            if start < high and start + 12 >= low:
-
-                @pl.when((j >= start) & (j <= start + 12) & (((j - start) & 3) == 0))
-                def _():
-                    y_sum((j - start) >> 2, s)
-
         for step, names in STEPS.items():
             if low <= step < high:
 
                 @pl.when(j == step)
                 def _():
-                    for name in names:
+                    for name in names.split():
                         actions[name]()
 
     own_cot.start()
-    rows = [((z + oz) & 3) << 11 for oz in ORDER]
-    places = [((y + oy) & 3) << 9 for oy in ORDER]
-    loads = [load_pair(4 * g + i, pl.multiple_of(rows[g] + places[i], 512)) for g in range(4) for i in range(4)]
+    rows = [((z + d) & 3) << 11 for d in range(4)]
+    places = [((y + d) & 3) << 9 for d in range(4)]
+    loads = [load_pair(SLOT[oz, oy], pl.multiple_of(rows[oz] + places[oy], 512)) for oz, oy in SEQUENCE]
     loads[0].start()
     own_w.start()
     for load in loads[1:]:
@@ -319,9 +307,9 @@
     def first_loop(j, carry):
         gradient(j)
 
-        @pl.when(j >= 2)
+        @pl.when(j >= 3)
         def _():
-            add_partner(j - 2)
+            add_partner(j - 3)
 
         events(j, 0, 16)
         return carry
@@ -331,38 +319,19 @@
     par[...] = jnp.zeros_like(par)
 
     def second_loop(j, carry):
-        @pl.when(j < 18)
+        @pl.when(j < 19)
         def _():
-            add_partner(j - 2)
+            add_partner(j - 3)
 
         events(j, 16, LAST)
 
-        @pl.when((j >= PROJECT) & (j < PROJECT + 4))
+        @pl.when((j >= PROJECT) & (j < PROJECT + 16))
         def _():
             project(15 + PROJECT - j)
 
         return carry
 
     lax.fori_loop(16, LAST, second_loop, 0)
-    update()
-
-    def near_loop(k, carry):
-        base = 12 - 4 * k
-        gather_y_near(base)
-
-        def three(i, inner):
-            project(base + 3 - i)
-            return inner
-
-        return lax.fori_loop(0, 3, three, carry)
-
-    def far_loop(k, carry):
-        gather_y_far(12 - 4 * k)
-        project(12 - 4 * k)
-        return carry
-
-    lax.fori_loop(1, 4, near_loop, 0)
-    lax.fori_loop(1, 4, far_loop, 0)
     kv[...] = acc[...].astype(jnp.bfloat16)
 
     def member(d, carry):
@@ -387,37 +356,49 @@
         partner_copy(slot).wait_send()
         return carry
 
-    def sent_group(g, carry):
-        for way in range(2):
-            y_copy(4 * g, 3, way).wait_send()
-            y_copy(4 * g, 1 + way, way).wait_send()
+    lax.fori_loop(0, 16, sent_slot, 0)
+    for way in range(2):
+        for g in range(4):
+            y_copy(g, 0, way).wait_send()
+            y_copy(g, 3 if way == 0 else 1, way).wait_send()
             for s in range(3):
                 ysum_copy(way, g, s).wait_send()
-        return carry
-
-    lax.fori_loop(0, 16, sent_slot, 0)
-    lax.fori_loop(0, 4, sent_group, 0)
-    for way in range(2):
-        z_copy(15, way).wait_send()
-        z_copy(7 if way == 0 else 11, way).wait_send()
+        z_copy(0, way).wait_send()
+        z_copy(3 if way == 0 else 1, way).wait_send()
         for s in range(3):
             zsum_copy(way, s).wait_send()
     lax.fori_loop(1, 16, lambda d, c: (p_copy(d).wait_send(), c)[1], 0)
 
 
-Y_STEPS = (2, 4, 6, 10)
 STEPS = {
-    5: ("near_0",),
-    8: ("z_near", "moments"),
-    9: ("far_0",),
-    10: ("z_antipode",),
-    13: ("z_far",),
-    14: ("z_free_1",),
-    16: ("z_joined_1",),
-    18: ("z_free_0", "z_joined_0", "spread_1", "spread_2", "spread_3"),
+    3: "y_0_0",
+    6: "y_0_1",
+    8: "y_2_0",
+    10: "y_1_0",
+    11: "y_0_2 near_0",
+    13: "y_2_1 y_1_1",
+    15: "moments",
+    16: "y_0_3",
+    17: "y_3_0",
+    18: "z_near",
+    19: "y_2_2",
+    21: "z_0",
+    22: "far_0 y_1_2",
+    24: "spread_3",
+    27: "y_3_2",
+    28: "spread_1 y_2_3",
+    29: "y_3_1 z_1",
+    30: "z_far y_1_3",
+    31: "z_2",
+    32: "spread_2 near_3 near_1",
+    33: "y_3_3",
+    34: "near_2 update",
+    35: "far_3",
+    36: "far_1",
+    37: "far_2",
 }
-PROJECT = 17
-LAST = 23
+PROJECT = 26
+LAST = 42
 
 
 def hand_out(*refs):
@@ -448,8 +429,7 @@
             pltpu.VMEM((256, 1024), jnp.bfloat16),
             pltpu.VMEM((2, 256, 256), jnp.float32),
             pltpu.VMEM((2, 256, 256), jnp.float32),
-            pltpu.VMEM((16, 256, 256), jnp.float32),
-            pltpu.VMEM((2, 256, 256), jnp.float32),
+            pltpu.VMEM((16, 2, 256, 256), jnp.float32),
             pltpu.VMEM((16, 272, 256), jnp.int16),
             pltpu.VMEM((16, 272, 256), jnp.int16),
             pltpu.VMEM((2, 4, 3, 272, 128), jnp.int16),

time: 58.2 us -> 53.8 us (0.924)
  Pallas kernels: 57.5 us -> 53.1 us
    pallas_call x1, Pallas kernels: 56.4 us -> 52.1 us  [local(): pl.pallas_call(kernel, out_shape=shapes, in_specs=[hbm] * 6, out_specs=(v...]
where the time goes in v3:
time: 53.8 us
  Pallas kernels  53.1 us (99%)
  between operations  0.64 us (1%)
    pallas_call x1, Pallas kernels, local(): pl.pallas_call(kernel, out_shape=shapes, in_specs=[hbm] * 6, out_specs=(v...  52.1 us
    pallas_call x1, Pallas kernels, local(): pl.pallas_call(hand_out, out_shape=shapes, in_specs=[vmem] * 4, out_specs...  1.08 us

profile of v3, /device:TPU:1, one launch (start us, length us, event | category | flops | bytes accessed | tf_op | source)
XLA Modules:
  0.0 53.8 jit_solution(10529928999874968570)
XLA Ops:
  0.6 52.1 %shard_map.93 = (bf16[1024,256]{1,0:T(8,128)(2,1)S(1)}, f32[256,256]{1,0:T(8,128)S(1)}, f32[256,256]{1,0:T(8,128)S(1)}, f32[4,2,32,128]{3,2,1,0:T(8,128)S(1)}) custom-call(bf16[1024,8192]{1,0:T(8,128)(2,1)} %normed.1, bf16[256,256]{1,0:T(8,128)(2,1)} %w.1, bf16[1024,256]{1,0:T(8,128)(2,1)} %cot.1, f32[256,256]{1,0:T(8,128)} %m1.1, f32[256,256]{1,0:T(8,128)} %m2.1, ...), custom_call_target="tpu_custom_call" | custom-call | tf_op jit(solution)/shard_map/pallas_call | solution.py:420
  52.7 1.1 %shard_map.94 = (bf16[1024,256]{1,0:T(8,128)(2,1)}, f32[256,256]{1,0:T(8,128)}, f32[256,256]{1,0:T(8,128)}, f32[4,2,32,128]{3,2,1,0:T(8,128)}) custom-call(bf16[1024,256]{1,0:T(8,128)(2,1)S(1)} %get-tuple-element.12.refs_0_, f32[256,256]{1,0:T(8,128)S(1)} %get-tuple-element.13.refs_1_, f32[256,256]{1,0:T(8,128)S(1)} %get-tuple-element.14.refs_2_, ...), custom_call_target="tpu_custom_call" | custom-call | tf_op jit(solution)/shard_map/pallas_call | solution.py:463
